TPU v7x, 32 devices: a whole 2x2x4 slice. The times are simulated.
32 devices in a mesh: dom: 8 (over z, core), grp: 4 (over y, x).
Axes of the slice: x: 2, y: 2, z: 4, core: 2. Of those that a mesh axis runs over, the one named last changes fastest.
Arguments:
- feats: bfloat16 [8192, 256], P(('dom', 'grp')), may hold values from -6 to 6
- w_self: bfloat16 [256, 256], replicated, may hold values from -0.375 to 0.375
- w_neigh: bfloat16 [256, 256], replicated, may hold values from -0.375 to 0.375
- local_tiles: bfloat16 [64, 3, 128, 128], P(('dom', 'grp')), may hold values from -0.15625 to 0.15625
- local_cols: int32 [64, 3], P(('dom', 'grp')), may hold values from 0 to 7, as said below
- cut_tiles: bfloat16 [64, 10, 128, 128], P(('dom', 'grp')), may hold values from -0.15625 to 0.15625
- cut_src: int32 [64, 10], P(('dom', 'grp')), may hold values from 0 to 7, as said below
- send_block: int32 [32, 8], P(('dom', 'grp')), may hold values from 0 to 1
- send_live: int32 [32, 8], P(('dom', 'grp')), may hold values from 0 to 1, as said below
- cotangent: bfloat16 [8192, 256], P(('dom', 'grp')), may hold values from -0.0625 to 0.0625
Outputs:
- layer_out: bfloat16 [8192, 256], P(('dom', 'grp'))
- grad_self: float32 [256, 256], replicated
- grad_neigh: float32 [256, 256], replicated
Inputs may be any that keep to these rules, and one draw needn't show every extreme that they name: `local_cols`: the 3 column blocks of one row block are distinct. `cut_src`: 0 marks an empty slot; the share of filled slots differs from partition to partition. send_live[e, p] is 1 exactly when some row block of device p * 4 + g (g the position of e) has a cut slot with offset naming e's partition; it is 0 where p is e's own partition.
All inputs are finite; a program needn't handle non-finite values.
Results may differ from a plain program's by a relative error of at most 0.0056.
Values may be sent and summed in bfloat16 or wider, within the bound.
A program may use at most 64 MiB of HBM per device.

v0:
```python
import jax
import jax.numpy as jnp
from jax import lax
from jax.sharding import PartitionSpec as P


def body(
    feats,
    w_self,
    w_neigh,
    local_tiles,
    local_cols,
    cut_tiles,
    cut_src,
    send_block,
    send_live,
    cotangent,
):
    row_blocks = local_tiles.shape[0]
    block_size = local_tiles.shape[2]
    features = feats.shape[1]
    partitions = lax.axis_size("dom")
    own_blocks = feats.reshape(row_blocks, block_size, features)
    gathered = lax.all_gather(feats, "grp", axis=0, tiled=True)
    picked = gathered.reshape(-1, block_size, features)[local_cols]
    aggregate_sum = jnp.einsum(
        "rkij,rkjf->rif", local_tiles, picked, preferred_element_type=jnp.float32
    )
    outgoing = own_blocks[send_block[0]] * send_live[0][:, None, None].astype(jnp.bfloat16)
    received = lax.all_to_all(outgoing, "dom", split_axis=0, concat_axis=0, tiled=True)
    source = (lax.axis_index("dom") + cut_src) % partitions
    remote = received[source]
    aggregate_sum = aggregate_sum + jnp.einsum(
        "rkij,rkjf->rif", cut_tiles, remote, preferred_element_type=jnp.float32
    )
    agg = aggregate_sum.reshape(row_blocks * block_size, features).astype(jnp.bfloat16)
    preact = jnp.dot(feats, w_self, preferred_element_type=jnp.float32) + jnp.dot(
        agg, w_neigh, preferred_element_type=jnp.float32
    )
    sigmoid = jax.nn.sigmoid(preact)
    layer_out = (preact * sigmoid).astype(jnp.bfloat16)
    grad_pre = (cotangent.astype(jnp.float32) * sigmoid * (1.0 + preact * (1.0 - sigmoid))).astype(
        jnp.bfloat16
    )
    grad_own = jnp.dot(feats.T, grad_pre, preferred_element_type=jnp.float32)
    grad_agg = jnp.dot(agg.T, grad_pre, preferred_element_type=jnp.float32)
    stacked = jnp.concatenate([grad_own, grad_agg], axis=0)
    shared = lax.psum_scatter(stacked, "grp", scatter_dimension=0, tiled=True)
    shared = lax.psum(shared, "dom")
    summed = lax.all_gather(shared, "grp", axis=0, tiled=True)
    return (layer_out, summed[:features], summed[features:])


def solution(mesh):
    return jax.shard_map(
        body,
        mesh=mesh,
        in_specs=(
            P(("dom", "grp"), None),
            P(),
            P(),
            P(("dom", "grp"), None, None, None),
            P(("dom", "grp"), None),
            P(("dom", "grp"), None, None, None),
            P(("dom", "grp"), None),
            P(("dom", "grp"), None),
            P(("dom", "grp"), None),
            P(("dom", "grp"), None),
        ),
        out_specs=(P(("dom", "grp"), None), P(), P()),
        check_vma=False,
    )
```

profile of v0, /device:TPU:0, one launch (start us, length us, event | category | flops | bytes accessed | tf_op | source)
XLA Modules:
  0.0 135.9 jit_solution(555693463951138174)
XLA Ops:
  7.2 0.0 copy-start
  7.2 0.7 fusion.3
  7.9 0.7 convert_bitcast_fusion
  8.6 1.5 %gather_fusion.1 = bf16[8,128,256]{2,1,0:T(8,128)(2,1)S(1)} fusion(bf16[2,128,256]{2,1,0:T(8,128)(2,1)} %bitcast.37, s32[1024]{0:T(1024)S(1)} %pad_clamp_fusion.1), kind=kCustom, calls=%fused_computation.1 | custom fusion | bytes 1048608 | tf_op jit(solution)/shard_map/gather | solution.py:29
  10.1 0.0 copy-start.4
  10.1 0.0 copy-start.5
  10.1 0.0 copy-start.1
  10.1 0.9 broadcast_multiply_fusion
  11.0 0.0 copy-start.2
  11.0 6.5 %all-to-all-start = ((bf16[8,128,256]{2,1,0:T(8,128)(2,1)}), bf16[8,128,256]{2,1,0:T(8,128)(2,1)S(1)}, u32[]{:S(2)}, u32[]{:S(2)}) async-start(bf16[8,128,256]{2,1,0:T(8,128)(2,1)} %broadcast_multiply_fusion), calls=%async_computation | async-start | bytes 1048576 | tf_op jit(solution)/shard_map/all_to_all | solution.py:30
  17.5 0.0 copy-start.3
  17.5 0.0 reduce-scatter.2.cloned.1.call-start
  17.5 0.0 copy-done.4
  17.6 0.1 reshape.70
  17.6 0.0 copy-done.5
  17.6 0.1 reshape.54
  17.7 0.0 copy-done.1
  17.7 10.6 %all_gather.6 = bf16[1024,256]{1,0:T(8,128)(2,1)S(1)} all-gather(bf16[256,256]{1,0:T(8,128)(2,1)S(1)} %copy-done.1), channel_id=1, replica_groups=mesh['dom'=8,'grp'=4] {'grp'}, dimensions={0}, use_global_device_ids=true | all-gather | bytes 655360 | tf_op jit(solution)/shard_map/all_gather | solution.py:24
  28.3 0.6 gather_fusion
  28.9 0.0 copy-done.2
  28.9 0.2 convolution_bitcast_fusion
  29.2 0.0 copy-done.3
  29.2 0.2 fusion.5
  29.4 3.5 %all-to-all-done = bf16[8,128,256]{2,1,0:T(8,128)(2,1)S(1)} async-done(((bf16[8,128,256]{2,1,0:T(8,128)(2,1)}), bf16[8,128,256]{2,1,0:T(8,128)(2,1)S(1)}, u32[]{:S(2)}, u32[]{:S(2)}) %all-to-all-start) | async-done | bytes 524320 | tf_op jit(solution)/shard_map/all_to_all | solution.py:30
  32.8 0.6 gather_fusion.2
  33.5 0.0 copy-start.6
  33.5 0.0 copy-start.7
  33.5 0.0 copy-done
  33.5 0.3 fusion.1
  33.9 0.5 copy-done.6
  34.4 0.1 copy-done.7
  34.4 0.9 multiply_convert_fusion
  35.4 0.2 fusion.6
  35.6 0.2 convolution_bitcast_fusion.1
  35.8 0.8 pad_maximum_fusion
  36.7 0.0 reduce-scatter.2.cloned.1.call-update
  36.7 0.0 all-reduce.2.cloned.1.call-start
  36.8 23.8 %reduce-scatter.2.cloned.1.call-done = f32[128,256]{1,0:T(8,128)} async-done(((f32[512,256]{1,0:T(8,128)}), f32[128,256]{1,0:T(8,128)}) %reduce-scatter.2.cloned.1.call-update) | async-done | bytes 131088 | tf_op jit(solution)/shard_map/reduce_scatter | solution.py:48
  60.5 0.0 all-reduce.2.cloned.1.call-update
  60.6 56.7 %all-reduce.2.cloned.1.call-done = f32[128,256]{1,0:T(8,128)} async-done(((f32[128,256]{1,0:T(8,128)}), f32[128,256]{1,0:T(8,128)}) %all-reduce.2.cloned.1.call-update) | async-done | bytes 131088 | tf_op jit(solution)/shard_map/psum | solution.py:49
  117.2 11.0 %all_gather.7 = f32[512,256]{1,0:T(8,128)S(1)} all-gather(f32[128,256]{1,0:T(8,128)} %all-reduce.2.cloned.1.call-done), channel_id=1, replica_groups=mesh['dom'=8,'grp'=4] {'grp'}, dimensions={0}, use_global_device_ids=true | all-gather | bytes 655360 | tf_op jit(solution)/shard_map/all_gather | solution.py:50
  128.3 0.8 fusion.4
  (5 shorter events, 0.0 us)
Async XLA Ops:
  7.2 26.3 %copy-start = (bf16[2,10,128,128]{3,2,1,0:T(8,128)(2,1)S(1)}, bf16[2,10,128,128]{3,2,1,0:T(8,128)(2,1)}, u32[]{:S(2)}) copy-start(bf16[2,10,128,128]{3,2,1,0:T(8,128)(2,1)} %param.15) | copy-start | bytes 1966084
  10.1 7.5 %copy-start.4 = (s32[2,10]{1,0:T(2,128)S(1)}, s32[2,10]{1,0:T(2,128)}, u32[]{:S(2)}) copy-start(s32[2,10]{1,0:T(2,128)} %param.16) | copy-start | bytes 244
  10.1 7.6 %copy-start.5 = (s32[2,3]{1,0:T(2,128)S(1)}, s32[2,3]{1,0:T(2,128)}, u32[]{:S(2)}) copy-start(s32[2,3]{1,0:T(2,128)} %param.14) | copy-start | bytes 76
  10.1 7.6 %copy-start.1 = (bf16[256,256]{1,0:T(8,128)(2,1)S(1)}, bf16[256,256]{1,0:T(8,128)(2,1)}, u32[]{:S(2)}) copy-start(bf16[256,256]{1,0:T(8,128)(2,1)} %param.10) | copy-start | bytes 393220
  11.0 17.9 %copy-start.2 = (bf16[2,3,128,128]{3,2,1,0:T(8,128)(2,1)S(1)}, bf16[2,3,128,128]{3,2,1,0:T(8,128)(2,1)}, u32[]{:S(2)}) copy-start(bf16[2,3,128,128]{3,2,1,0:T(8,128)(2,1)} %param.13) | copy-start | bytes 589828
  11.0 21.8 %all-to-all-start = ((bf16[8,128,256]{2,1,0:T(8,128)(2,1)}), bf16[8,128,256]{2,1,0:T(8,128)(2,1)S(1)}, u32[]{:S(2)}, u32[]{:S(2)}) async-start(bf16[8,128,256]{2,1,0:T(8,128)(2,1)} %broadcast_multiply_fusion), calls=%async_computation | async-start | bytes 1048576 | tf_op jit(solution)/shard_map/all_to_all | solution.py:30
  17.5 11.7 %copy-start.3 = (bf16[256,256]{1,0:T(8,128)(2,1)S(1)}, bf16[256,256]{1,0:T(8,128)(2,1)}, u32[]{:S(2)}) copy-start(bf16[256,256]{1,0:T(8,128)(2,1)} %param.11) | copy-start | bytes 393220
  17.5 43.1 %reduce-scatter.2.cloned.1.call-start = ((), (), s32[]{:S(2)}) async-start(), calls=%async_computation.2 | async-start | bytes 655360 | tf_op jit(solution)/shard_map/reduce_scatter | solution.py:48
  33.5 0.9 copy-start.6
  33.5 1.0 copy-start.7
  36.7 80.5 %all-reduce.2.cloned.1.call-start = ((), (), s32[]{:S(2)}) async-start(), calls=%async_computation.3 | async-start | bytes 262144 | tf_op jit(solution)/shard_map/psum | solution.py:49
Sparse Core Ops, SparseCore 0:
  36.8 23.6 reduce-scatter.1
  63.0 54.2 all-reduce.1
where the time goes:
time: 136 us
  waiting for transfers between devices  84 us (62%)
  blocking collectives  21.6 us (16%)
  between operations  14.2 us (10%)
  starting transfers between devices  6.54 us (5%)
  local copies, waits for them, and re-layouts  4.3 us (3%)
  other arithmetic  3.17 us (2%)
  matrix products  2.14 us (2%)
    psum x1, waiting for transfers between devices, body(): shared = lax.psum(shared, 'dom')  56.7 us
    reduce_scatter x1, waiting for transfers between devices, body(): shared = lax.psum_scatter(stacked, 'grp', scatter_dimension=0, tiled=True)  23.8 us
    all_gather x1, blocking collectives, body(): summed = lax.all_gather(shared, 'grp', axis=0, tiled=True)  11 us
    all_gather x1, blocking collectives, body(): gathered = lax.all_gather(feats, 'grp', axis=0, tiled=True)  10.6 us
    all_to_all x1, starting transfers between devices, body(): lax.all_to_all(outgoing, 'dom', split_axis=0, concat_axis=0, tiled=True)  6.46 us
    all_to_all x1, waiting for transfers between devices, body(): lax.all_to_all(outgoing, 'dom', split_axis=0, concat_axis=0, tiled=True)  3.46 us
  transfers between devices with their start and end apart: 3, of which 3 were waited for; matrix products, arithmetic and copies ran while one was open for 1% of the time, Pallas kernels for 0%

commit v1 on v0

--- a/solution.py
+++ b/solution.py
@@ -27,7 +27,19 @@
         "rkij,rkjf->rif", local_tiles, picked, preferred_element_type=jnp.float32
     )
     outgoing = own_blocks[send_block[0]] * send_live[0][:, None, None].astype(jnp.bfloat16)
-    received = lax.all_to_all(outgoing, "dom", split_axis=0, concat_axis=0, tiled=True)
+    ways, here = (lax.axis_size("dom"), lax.axis_index("dom"))
+    width = outgoing.shape[0] // ways
+    shape = list(outgoing.shape)
+    shape[0] = width
+    height = shape[0]
+    shape[0] = height * ways
+    full = jnp.zeros(shape, outgoing.dtype)
+    for mask in range(ways):
+        part = lax.dynamic_slice_in_dim(outgoing, (here ^ mask) * width, width, axis=0)
+        if mask:
+            part = lax.ppermute(part, "dom", [(d, d ^ mask) for d in range(ways)])
+        full = lax.dynamic_update_slice_in_dim(full, part, (here ^ mask) * height, axis=0)
+    received = full
     source = (lax.axis_index("dom") + cut_src) % partitions
     remote = received[source]
     aggregate_sum = aggregate_sum + jnp.einsum(

time: 136 us -> 141 us (1.037)
  starting transfers between devices: 6.54 us -> 9.81 us
  local copies, waits for them, and re-layouts: 4.3 us -> 6.99 us
    ppermute x0 -> x7, starting transfers between devices: none -> 9.73 us  [body(): part = lax.ppermute(part, 'dom', [(d, d ^ mask) for d in range(ways)])]
    all_to_all x1 -> x0, starting transfers between devices: 6.46 us -> none  [body(): lax.all_to_all(outgoing, 'dom', split_axis=0, concat_axis=0, tiled=True)]
    ppermute x0 -> x7, waiting for transfers between devices: none -> 3.71 us  [body(): part = lax.ppermute(part, 'dom', [(d, d ^ mask) for d in range(ways)])]
    all_to_all x1 -> x0, waiting for transfers between devices: 3.46 us -> none  [body(): lax.all_to_all(outgoing, 'dom', split_axis=0, concat_axis=0, tiled=True)]
    dynamic_update_slice x0 -> x7, local copies, waits for them, and re-layouts: none -> 2.58 us  [body(): lax.dynamic_update_slice_in_dim(full, part, (here ^ mask) * height, axis=0)]
  transfers between devices with their start and end apart: 3 -> 9, of which waited for: 3 -> 3; matrix products, arithmetic and copies ran while one was open for 1% -> 3% of each run, Pallas kernels for 0% -> 0%
where the time goes in v1:
time: 141 us; the launch traced here: 140 us
  waiting for transfers between devices  83 us (59%)
  blocking collectives  21.6 us (15%)
  between operations  14.3 us (10%)
  starting transfers between devices  9.81 us (7%)
  local copies, waits for them, and re-layouts  6.99 us (5%)
  other arithmetic  2.35 us (2%)
  matrix products  2.13 us (2%)
    psum x1, waiting for transfers between devices, body(): shared = lax.psum(shared, 'dom')  56.7 us
    reduce_scatter x1, waiting for transfers between devices, body(): shared = lax.psum_scatter(stacked, 'grp', scatter_dimension=0, tiled=True)  22.6 us
    all_gather x1, blocking collectives, body(): summed = lax.all_gather(shared, 'grp', axis=0, tiled=True)  11 us
    all_gather x1, blocking collectives, body(): gathered = lax.all_gather(feats, 'grp', axis=0, tiled=True)  10.6 us
    ppermute x7, starting transfers between devices, body(): part = lax.ppermute(part, 'dom', [(d, d ^ mask) for d in range(ways)])  9.73 us
    ppermute x7, waiting for transfers between devices, body(): part = lax.ppermute(part, 'dom', [(d, d ^ mask) for d in range(ways)])  3.71 us
  transfers between devices with their start and end apart: 9, of which 3 were waited for; matrix products, arithmetic and copies ran while one was open for 3% of the time, Pallas kernels for 0%

profile of v1, /device:TPU:0, one launch (start us, length us, event | category | flops | bytes accessed | tf_op | source)
XLA Modules:
  0.0 140.1 jit_solution(15270233014226268415)
XLA Ops:
  7.2 0.0 copy-start
  7.2 0.0 reduce-scatter.2.cloned.1.call-start
  7.3 0.7 fusion.3
  8.0 0.7 convert_bitcast_fusion
  8.6 1.5 %gather_fusion.1 = bf16[8,128,256]{2,1,0:T(8,128)(2,1)S(1)} fusion(bf16[2,128,256]{2,1,0:T(8,128)(2,1)} %bitcast.37, s32[1024]{0:T(1024)S(1)} %pad_clamp_fusion.1), kind=kCustom, calls=%fused_computation.1 | custom fusion | bytes 1048608 | tf_op jit(solution)/shard_map/gather | solution.py:29
  10.1 0.0 copy-start.1
  10.1 0.1 broadcast_multiply_fusion
  10.2 0.0 copy-start.4
  10.3 0.0 copy-start.5
  10.3 0.0 copy-start.3
  10.3 0.0 copy-start.2
  10.3 0.1 constant_dynamic-slice_fusion
  10.4 0.5 collective-permute-start
  10.9 2.7 %collective-permute-start.1 = (bf16[1,128,256]{2,1,0:T(8,128)(2,1)S(1)}, bf16[1,128,256]{2,1,0:T(8,128)(2,1)}, u32[]{:S(2)}, u32[]{:S(2)}) collective-permute-start(bf16[1,128,256]{2,1,0:T(8,128)(2,1)S(1)} %get-tuple-element.10), channel_id=1, source_target_pairs={{0,8},{4,12},{8,0},{12,4},{16,24},{20,28},{24,16},{28,20},{1,9},{5... | collective-permute-start | bytes 196616 | tf_op jit(solution)/shard_map/ppermute | solution.py:40
  13.6 0.1 collective-permute-start.2
  13.6 2.8 %collective-permute-start.3 = (bf16[1,128,256]{2,1,0:T(8,128)(2,1)S(1)}, bf16[1,128,256]{2,1,0:T(8,128)(2,1)S(1)}, u32[]{:S(2)}, u32[]{:S(2)}) collective-permute-start(bf16[1,128,256]{2,1,0:T(8,128)(2,1)S(1)} %get-tuple-element.8), channel_id=1, source_target_pairs={{0,16},{4,20},{8,24},{12,28},{16,0},{20,4},{24,8},{28,12},{1,17},{... | collective-permute-start | bytes 196616 | tf_op jit(solution)/shard_map/ppermute | solution.py:40
  16.4 0.0 collective-permute-start.4
  16.4 10.6 %all_gather.6 = bf16[1024,256]{1,0:T(8,128)(2,1)S(1)} all-gather(bf16[256,256]{1,0:T(8,128)(2,1)S(1)} %copy-done.1), channel_id=1, replica_groups=mesh['dom'=8,'grp'=4] {'grp'}, dimensions={0}, use_global_device_ids=true | all-gather | bytes 655360 | tf_op jit(solution)/shard_map/all_gather | solution.py:24
  27.0 0.1 reshape.70
  27.1 0.1 reshape.54
  27.2 0.2 fusion.5
  27.4 0.6 gather_fusion
  28.0 0.2 convolution_bitcast_fusion
  28.2 3.7 %collective-permute-start.5 = (bf16[1,128,256]{2,1,0:T(8,128)(2,1)S(1)}, bf16[1,128,256]{2,1,0:T(8,128)(2,1)S(1)}, u32[]{:S(2)}, u32[]{:S(2)}) collective-permute-start(bf16[1,128,256]{2,1,0:T(8,128)(2,1)S(1)} %get-tuple-element.6), channel_id=1, source_target_pairs={{0,24},{4,28},{8,16},{12,20},{16,8},{20,12},{24,0},{28,4},{1,25},{... | collective-permute-start | bytes 196616 | tf_op jit(solution)/shard_map/ppermute | solution.py:40
  31.9 0.8 constant_dynamic-update-slice_fusion.6
  32.7 0.1 collective-permute-start.6
  32.8 0.9 constant_dynamic-update-slice_fusion.5
  33.7 0.0 collective-permute-done.2
  33.7 0.8 constant_dynamic-update-slice_fusion.4
  34.5 0.0 collective-permute-done.3
  34.6 3.7 %collective-permute-done.6 = bf16[1,128,256]{2,1,0:T(8,128)(2,1)S(1)} collective-permute-done((bf16[1,128,256]{2,1,0:T(8,128)(2,1)S(1)}, bf16[1,128,256]{2,1,0:T(8,128)(2,1)S(1)}, u32[]{:S(2)}, u32[]{:S(2)}) %collective-permute-start.6) | collective-permute-done | bytes 65568 | tf_op jit(solution)/shard_map/ppermute | solution.py:40
  38.3 0.6 gather_fusion.2
  38.9 0.0 copy-start.6
  39.0 0.0 copy-start.7
  39.0 0.3 fusion.1
  39.3 0.5 copy-done.6
  39.8 0.1 copy-done.7
  39.9 0.9 multiply_convert_fusion
  40.9 0.2 convolution_bitcast_fusion.1
  41.1 0.2 fusion.6
  41.3 0.8 pad_maximum_fusion
  42.2 0.0 reduce-scatter.2.cloned.1.call-update
  42.2 0.0 all-reduce.2.cloned.1.call-start
  42.2 22.6 %reduce-scatter.2.cloned.1.call-done = f32[128,256]{1,0:T(8,128)} async-done(((f32[512,256]{1,0:T(8,128)}), f32[128,256]{1,0:T(8,128)}) %reduce-scatter.2.cloned.1.call-update) | async-done | bytes 131088 | tf_op jit(solution)/shard_map/reduce_scatter | solution.py:60
  64.8 0.0 all-reduce.2.cloned.1.call-update
  64.8 56.7 %all-reduce.2.cloned.1.call-done = f32[128,256]{1,0:T(8,128)} async-done(((f32[128,256]{1,0:T(8,128)}), f32[128,256]{1,0:T(8,128)}) %all-reduce.2.cloned.1.call-update) | async-done | bytes 131088 | tf_op jit(solution)/shard_map/psum | solution.py:61
  121.5 11.0 %all_gather.7 = f32[512,256]{1,0:T(8,128)S(1)} all-gather(f32[128,256]{1,0:T(8,128)} %all-reduce.2.cloned.1.call-done), channel_id=1, replica_groups=mesh['dom'=8,'grp'=4] {'grp'}, dimensions={0}, use_global_device_ids=true | all-gather | bytes 655360 | tf_op jit(solution)/shard_map/all_gather | solution.py:62
  132.5 0.8 fusion.4
  (20 shorter events, 0.1 us)
Async XLA Ops:
  7.2 31.8 %copy-start = (bf16[2,10,128,128]{3,2,1,0:T(8,128)(2,1)S(1)}, bf16[2,10,128,128]{3,2,1,0:T(8,128)(2,1)}, u32[]{:S(2)}) copy-start(bf16[2,10,128,128]{3,2,1,0:T(8,128)(2,1)} %param.15) | copy-start | bytes 1966084
  7.2 57.6 %reduce-scatter.2.cloned.1.call-start = ((), (), s32[]{:S(2)}) async-start(), calls=%async_computation.1 | async-start | bytes 655360 | tf_op jit(solution)/shard_map/reduce_scatter | solution.py:60
  10.1 6.3 %copy-start.1 = (bf16[256,256]{1,0:T(8,128)(2,1)S(1)}, bf16[256,256]{1,0:T(8,128)(2,1)}, u32[]{:S(2)}) copy-start(bf16[256,256]{1,0:T(8,128)(2,1)} %param.10) | copy-start | bytes 393220
  10.2 16.7 %copy-start.4 = (s32[2,10]{1,0:T(2,128)S(1)}, s32[2,10]{1,0:T(2,128)}, u32[]{:S(2)}) copy-start(s32[2,10]{1,0:T(2,128)} %param.16) | copy-start | bytes 244
  10.3 16.8 %copy-start.5 = (s32[2,3]{1,0:T(2,128)S(1)}, s32[2,3]{1,0:T(2,128)}, u32[]{:S(2)}) copy-start(s32[2,3]{1,0:T(2,128)} %param.14) | copy-start | bytes 76
  10.3 16.9 %copy-start.3 = (bf16[256,256]{1,0:T(8,128)(2,1)S(1)}, bf16[256,256]{1,0:T(8,128)(2,1)}, u32[]{:S(2)}) copy-start(bf16[256,256]{1,0:T(8,128)(2,1)} %param.11) | copy-start | bytes 393220
  10.3 17.6 %copy-start.2 = (bf16[2,3,128,128]{3,2,1,0:T(8,128)(2,1)S(1)}, bf16[2,3,128,128]{3,2,1,0:T(8,128)(2,1)}, u32[]{:S(2)}) copy-start(bf16[2,3,128,128]{3,2,1,0:T(8,128)(2,1)} %param.13) | copy-start | bytes 589828
  10.4 17.8 %collective-permute-start = (bf16[1,128,256]{2,1,0:T(8,128)(2,1)S(1)}, bf16[1,128,256]{2,1,0:T(8,128)(2,1)}, u32[]{:S(2)}, u32[]{:S(2)}) collective-permute-start(bf16[1,128,256]{2,1,0:T(8,128)(2,1)S(1)} %get-tuple-element.11), channel_id=1, source_target_pairs={{0,4},{4,0},{8,12},{12,8},{16,20},{20,16},{24,28},{28,24},{1,5},{5... | collective-permute-start | bytes 196616 | tf_op jit(solution)/shard_map/ppermute | solution.py:40
  10.9 21.8 %collective-permute-start.1 = (bf16[1,128,256]{2,1,0:T(8,128)(2,1)S(1)}, bf16[1,128,256]{2,1,0:T(8,128)(2,1)}, u32[]{:S(2)}, u32[]{:S(2)}) collective-permute-start(bf16[1,128,256]{2,1,0:T(8,128)(2,1)S(1)} %get-tuple-element.10), channel_id=1, source_target_pairs={{0,8},{4,12},{8,0},{12,4},{16,24},{20,28},{24,16},{28,20},{1,9},{5... | collective-permute-start | bytes 196616 | tf_op jit(solution)/shard_map/ppermute | solution.py:40
  13.6 20.1 %collective-permute-start.2 = (bf16[1,128,256]{2,1,0:T(8,128)(2,1)S(1)}, bf16[1,128,256]{2,1,0:T(8,128)(2,1)}, u32[]{:S(2)}, u32[]{:S(2)}) collective-permute-start(bf16[1,128,256]{2,1,0:T(8,128)(2,1)S(1)} %get-tuple-element.9), channel_id=1, source_target_pairs={{0,12},{4,8},{8,4},{12,0},{16,28},{20,24},{24,20},{28,16},{1,13},{... | collective-permute-start | bytes 196616 | tf_op jit(solution)/shard_map/ppermute | solution.py:40
  13.6 20.9 %collective-permute-start.3 = (bf16[1,128,256]{2,1,0:T(8,128)(2,1)S(1)}, bf16[1,128,256]{2,1,0:T(8,128)(2,1)S(1)}, u32[]{:S(2)}, u32[]{:S(2)}) collective-permute-start(bf16[1,128,256]{2,1,0:T(8,128)(2,1)S(1)} %get-tuple-element.8), channel_id=1, source_target_pairs={{0,16},{4,20},{8,24},{12,28},{16,0},{20,4},{24,8},{28,12},{1,17},{... | collective-permute-start | bytes 196616 | tf_op jit(solution)/shard_map/ppermute | solution.py:40
  16.4 18.1 %collective-permute-start.4 = (bf16[1,128,256]{2,1,0:T(8,128)(2,1)S(1)}, bf16[1,128,256]{2,1,0:T(8,128)(2,1)S(1)}, u32[]{:S(2)}, u32[]{:S(2)}) collective-permute-start(bf16[1,128,256]{2,1,0:T(8,128)(2,1)S(1)} %get-tuple-element.7), channel_id=1, source_target_pairs={{0,20},{4,16},{8,28},{12,24},{16,4},{20,0},{24,12},{28,8},{1,21},{... | collective-permute-start | bytes 196616 | tf_op jit(solution)/shard_map/ppermute | solution.py:40
  28.2 6.3 %collective-permute-start.5 = (bf16[1,128,256]{2,1,0:T(8,128)(2,1)S(1)}, bf16[1,128,256]{2,1,0:T(8,128)(2,1)S(1)}, u32[]{:S(2)}, u32[]{:S(2)}) collective-permute-start(bf16[1,128,256]{2,1,0:T(8,128)(2,1)S(1)} %get-tuple-element.6), channel_id=1, source_target_pairs={{0,24},{4,28},{8,16},{12,20},{16,8},{20,12},{24,0},{28,4},{1,25},{... | collective-permute-start | bytes 196616 | tf_op jit(solution)/shard_map/ppermute | solution.py:40
  32.7 5.5 %collective-permute-start.6 = (bf16[1,128,256]{2,1,0:T(8,128)(2,1)S(1)}, bf16[1,128,256]{2,1,0:T(8,128)(2,1)S(1)}, u32[]{:S(2)}, u32[]{:S(2)}) collective-permute-start(bf16[1,128,256]{2,1,0:T(8,128)(2,1)S(1)} %get-tuple-element.5), channel_id=1, source_target_pairs={{0,28},{4,24},{8,20},{12,16},{16,12},{20,8},{24,4},{28,0},{1,29},{... | collective-permute-start | bytes 196616 | tf_op jit(solution)/shard_map/ppermute | solution.py:40
  38.9 0.9 copy-start.6
  39.0 1.0 copy-start.7
  42.2 79.3 %all-reduce.2.cloned.1.call-start = ((), (), s32[]{:S(2)}) async-start(), calls=%async_computation.2 | async-start | bytes 262144 | tf_op jit(solution)/shard_map/psum | solution.py:61
Sparse Core Ops, SparseCore 0:
  42.3 22.4 reduce-scatter.1
  67.2 54.2 all-reduce.1
